TPU v7x, 512 devices: a whole 4x8x8 slice. The times are simulated.
512 devices in a mesh: grp: 64 (over x, z, core), tp: 8 (over y).
Axes of the slice: x: 4, y: 8, z: 8, core: 2. Of those that a mesh axis runs over, the one named last changes fastest.
Arguments:
- patches: bfloat16 [65536, 1280], P(('grp', 'tp')), may hold values from -6 to 6
- pictures: int32 [64, 1024], P('grp', 'tp'), may hold values from 0 to 1, as said below
- vis_qkv: bfloat16 [3, 1280, 1280], P(None, 'tp'), as said below
- vis_out: bfloat16 [1280, 1280], P(None, 'grp'), may hold values from -0.15625 to 0.15625
- merge_w: bfloat16 [1280, 5120], P('tp'), may hold values from -0.078125 to 0.078125
- text: bfloat16 [65536, 1280], P(('grp', 'tp')), may hold values from -6 to 6
- places: int32 [16384], P(('grp', 'tp')), may hold values from 0 to 65535, as said below
- segments: int32 [64, 1024], P('grp', 'tp'), may hold values from 0 to 3, never falling along the last dimension, each value on 1 to 512 neighbouring positions
- txt_qkv: bfloat16 [3, 1280, 1280], P(None, 'tp'), as said below
- txt_out: bfloat16 [1280, 1280], P(None, 'grp'), may hold values from -0.15625 to 0.15625
Outputs:
- hidden_out: bfloat16 [65536, 1280], P(('grp', 'tp'))
Inputs may be any that keep to these rules, and one draw needn't show every extreme that they name: `pictures`: within each row, picture numbers never fall; each picture is a run of whole aligned blocks of 4 positions and covers at least a quarter of the row, rounded down to whole blocks of 4 (at least one block). Row 0 holds one picture, row 1 two, the others one or two. `places`: all positions are distinct. The image rows of one device (aligned blocks of 32 rows, devices in the order of the placement) go to tokens held by the device of the same tp index in their token group: to 16 different token groups, exactly 2 rows to each. For each tp index, one token group receives 2 rows from every device of that tp index. `vis_qkv`: the query and key parts of a head may be correlated. `txt_qkv`: the query and key parts of a head may be correlated.
All inputs are finite; a program needn't handle non-finite values.
Results may differ from a plain program's by a relative error of at most 0.01.
Values may be sent and summed in bfloat16 or wider, within the bound.
A program may use at most 64 MiB of HBM per device.

v0:
```python
import jax
import jax.numpy as jnp
from jax import lax
from jax.sharding import PartitionSpec as P

HEAD_DIM = 80
SEND_CAP = 2
EPSILON = 1e-05
MASKED = -1e30


def layer_norm(rows):
    widened = rows.astype(jnp.float32)
    row_mean = jnp.mean(widened, axis=-1, keepdims=True)
    centred = widened - row_mean
    spread = jnp.mean(centred * centred, axis=-1, keepdims=True)
    return (centred * lax.rsqrt(spread + EPSILON)).astype(jnp.bfloat16)


def times_transpose(left, right):
    return lax.dot_general(
        left, right, (((1,), (1,)), ((), ())), preferred_element_type=jnp.float32
    )


def local_attention(queries, key_rows, value_rows, labels, causal):
    row_count, col_count = queries.shape
    heads_here = col_count // HEAD_DIM
    q_heads = queries.reshape(row_count, heads_here, HEAD_DIM)
    k_heads = key_rows.reshape(row_count, heads_here, HEAD_DIM)
    v_heads = value_rows.reshape(row_count, heads_here, HEAD_DIM)
    blocks = max(1, min(8, row_count // 512))
    block_rows = row_count // blocks
    inv_root = HEAD_DIM ** (-0.5)
    outputs = []
    for block_index in range(blocks):
        begin_row = block_index * block_rows
        end_key = begin_row + block_rows if causal else row_count
        scores = (
            jnp.einsum(
                "qhd,khd->hqk",
                q_heads[begin_row : begin_row + block_rows],
                k_heads[:end_key],
                preferred_element_type=jnp.float32,
            )
            * inv_root
        )
        allowed = labels[begin_row : begin_row + block_rows, None] == labels[None, :end_key]
        if causal:
            query_ids = jnp.arange(begin_row, begin_row + block_rows, dtype=jnp.int32)
            key_ids = jnp.arange(end_key, dtype=jnp.int32)
            allowed = allowed & (query_ids[:, None] >= key_ids[None, :])
        scores = jnp.where(allowed[None], scores, MASKED)
        row_max = jnp.max(scores, axis=-1, keepdims=True)
        weights = jnp.exp(scores - row_max)
        prob_bf = (weights / jnp.sum(weights, axis=-1, keepdims=True)).astype(jnp.bfloat16)
        mixed = jnp.einsum(
            "hqk,khd->qhd", prob_bf, v_heads[:end_key], preferred_element_type=jnp.float32
        )
        outputs.append(mixed.astype(jnp.bfloat16).reshape(block_rows, col_count))
    return jnp.concatenate(outputs, axis=0)


def attention_heads(gathered, weights, labels, causal):
    queries = times_transpose(gathered, weights[0]).astype(jnp.bfloat16)
    key_rows = times_transpose(gathered, weights[1]).astype(jnp.bfloat16)
    value_rows = times_transpose(gathered, weights[2]).astype(jnp.bfloat16)
    return local_attention(queries, key_rows, value_rows, labels, causal)


def project_out(rows_here, columns):
    return jnp.dot(
        rows_here,
        lax.all_gather(columns, "grp", axis=1, tiled=True),
        preferred_element_type=jnp.float32,
    )


def per_device(
    patches, pictures, vis_qkv, vis_out, merge_w, text, places, segments, txt_qkv, txt_out
):
    tp_count = lax.axis_size("tp")
    grp_count = lax.axis_size("grp")
    patch_normed = layer_norm(patches)
    group_rows, group_pics = (
        lax.all_gather(patch_normed, "tp", axis=0, tiled=True),
        lax.all_gather(pictures, "tp", axis=1, tiled=True),
    )
    heads_vis = attention_heads(group_rows, vis_qkv, group_pics[0], False)
    own_heads = lax.all_to_all(heads_vis, "tp", split_axis=0, concat_axis=1, tiled=True)
    vis_hidden = (patches.astype(jnp.float32) + project_out(own_heads, vis_out)).astype(
        jnp.bfloat16
    )
    merged = layer_norm(vis_hidden).reshape(patches.shape[0] // 4, 4 * patches.shape[1])
    image_cols = times_transpose(lax.all_gather(merged, "tp", axis=0, tiled=True), merge_w).astype(
        jnp.bfloat16
    )
    image_rows = lax.all_to_all(image_cols, "tp", split_axis=0, concat_axis=1, tiled=True)
    tok_count = text.shape[0]
    group_tokens = tok_count * tp_count
    dest_group = places // group_tokens
    dest_local = places % tok_count
    row_total = places.shape[0]
    row_ids = jnp.arange(row_total, dtype=jnp.int32)
    earlier = row_ids[:, None] > row_ids[None, :]
    same_dest = dest_group[:, None] == dest_group[None, :]
    slot_rank = jnp.sum((earlier & same_dest).astype(jnp.int32), axis=1)
    slot_index = dest_group * SEND_CAP + slot_rank
    slot_ids = jnp.arange(grp_count * SEND_CAP, dtype=jnp.int32)
    slot_pick = slot_ids[:, None] == slot_index[None, :]
    send_rows = jnp.dot(
        slot_pick.astype(jnp.bfloat16), image_rows, preferred_element_type=jnp.float32
    ).astype(jnp.bfloat16)
    send_pos = jnp.sum(jnp.where(slot_pick, dest_local[None, :] + 1, 0), axis=1) - 1
    send_rows = send_rows.reshape(grp_count, SEND_CAP, image_rows.shape[1])
    send_pos = send_pos.reshape(grp_count, SEND_CAP)
    recv_rows, recv_pos = (
        lax.all_to_all(send_rows, "grp", split_axis=0, concat_axis=0, tiled=True),
        lax.all_to_all(send_pos, "grp", split_axis=0, concat_axis=0, tiled=True),
    )
    recv_rows = recv_rows.reshape(grp_count * SEND_CAP, image_rows.shape[1])
    recv_pos = recv_pos.reshape(grp_count * SEND_CAP)
    position_hit = jnp.arange(tok_count, dtype=jnp.int32)[:, None] == recv_pos[None, :]
    placed = jnp.dot(
        position_hit.astype(jnp.bfloat16), recv_rows, preferred_element_type=jnp.float32
    ).astype(jnp.bfloat16)
    covered = jnp.any(position_hit, axis=1)
    prompt = jnp.where(covered[:, None], placed, text)
    token_normed = layer_norm(prompt)
    all_tokens, all_segments = (
        lax.all_gather(token_normed, "tp", axis=0, tiled=True),
        lax.all_gather(segments, "tp", axis=1, tiled=True),
    )
    heads_txt = attention_heads(all_tokens, txt_qkv, all_segments[0], True)
    own_text = lax.all_to_all(heads_txt, "tp", split_axis=0, concat_axis=1, tiled=True)
    return (prompt.astype(jnp.float32) + project_out(own_text, txt_out)).astype(jnp.bfloat16)


def solution(mesh):
    placed = (
        P(("grp", "tp"), None),
        P("grp", "tp"),
        P(None, "tp", None),
        P(None, "grp"),
        P("tp", None),
        P(("grp", "tp"), None),
        P(("grp", "tp")),
        P("grp", "tp"),
        P(None, "tp", None),
        P(None, "grp"),
    )
    return jax.shard_map(
        per_device, mesh=mesh, in_specs=placed, out_specs=P(("grp", "tp"), None), check_vma=False
    )
```

profile of v0, /device:TPU:1, one launch (start us, length us, event | category | flops | bytes accessed | tf_op | source)
XLA Modules:
  0.0 397.2 jit_solution(6746148892684774772)
XLA Ops:
  6.5 1.2 convert_reduce_fusion
  7.8 1.2 fusion.35
  9.0 1.9 fusion.36
  11.0 0.7 all-gather.14.cloned.1.call-update
  11.7 14.0 %all_gather.26 = s32[1,1024]{1,0:T(1,128)S(1)} all-gather(s32[1,128]{1,0:T(1,128)} %param.11), channel_id=1, replica_groups=mesh['grp'=64,'tp'=8] {'tp'}, dimensions={1}, use_global_device_ids=true | all-gather | bytes 4608 | tf_op jit(solution)/shard_map/all_gather | solution.py:87
  26.3 31.7 %all-gather.8.cloned.1.call-done = bf16[1024,1280]{1,0:T(8,128)(2,1)} async-done(((bf16[128,1280]{1,0:T(8,128)(2,1)}), bf16[1024,1280]{1,0:T(8,128)(2,1)}) %all-gather.8.cloned.1.call-update) | async-done | bytes 2621456 | tf_op jit(solution)/shard_map/all_gather | solution.py:86
  58.0 2.9 convolution_convert_fusion.6
  61.0 1.0 convolution_convert_fusion.7
  62.0 1.7 convolution_convert_fusion.5
  63.7 4.6 %fusion.79 = (f32[2,512]{1,0:T(2,128)S(1)}, f32[2,512,1024]{2,1,0:T(8,128)}) fusion(pred[512,1024]{1,0:T(8,128)(4,1)S(1)} %get-tuple-element.12, bf16[512,2,80]{0,2,1:T(8,128)(2,1)S(1)} %bitcast.111, bf16[1024,2,80]{0,2,1:T(8,128)(2,1)} %bitcast.132), kind=kOutput, calls=%fused_computation.131 | convolution fusion | flops 171967488 | bytes 5214208 | tf_op jit(solution)/shard_map/sub | solution.py:55
  68.3 4.6 %fusion.80 = (f32[2,512]{1,0:T(2,128)S(1)}, f32[2,512,1024]{2,1,0:T(8,128)}) fusion(pred[512,1024]{1,0:T(8,128)(4,1)S(1)} %get-tuple-element.11, bf16[512,2,80]{0,2,1:T(8,128)(2,1)S(1)} %bitcast.109, bf16[1024,2,80]{0,2,1:T(8,128)(2,1)} %bitcast.133), kind=kOutput, calls=%fused_computation.132 | convolution fusion | flops 171967488 | bytes 5214208 | tf_op jit(solution)/shard_map/sub | solution.py:55
  73.0 3.2 fusion.27
  76.4 0.8 fusion.28
  77.3 0.8 copy_bitcast_fusion.1
  78.1 4.0 %all-to-all-start.1 = ((bf16[8,128,160]{1,2,0:T(8,128)(2,1)}), bf16[8,128,160]{1,2,0:T(8,128)(2,1)S(1)}, u32[]{:S(2)}, u32[]{:S(2)}) async-start(bf16[8,128,160]{1,2,0:T(8,128)(2,1)} %copy_bitcast_fusion.1), calls=%async_computation.1 | async-start | bytes 655360 | tf_op jit(solution)/shard_map/all_to_all | solution.py:90
  82.1 66.2 %all-gather.14.cloned.1.call-done = bf16[64,20,1280]{2,1,0:T(8,128)(2,1)} async-done(((bf16[1,20,1280]{2,1,0:T(8,128)(2,1)}), bf16[64,20,1280]{2,1,0:T(8,128)(2,1)}) %all-gather.14.cloned.1.call-update) | async-done | bytes 3276816 | tf_op jit(solution)/shard_map/all_gather | solution.py:74
  148.4 6.1 %reshape.296 = bf16[1280,1280]{1,0:T(8,128)(2,1)} reshape(bf16[64,20,1280]{2,1,0:T(8,128)(2,1)} %all-gather.14.cloned.1.call-done) | data formatting | bytes 6553600
  154.5 3.2 fusion.81
  158.1 0.9 reshape.288
  159.4 37.7 %all-gather.10.cloned.1.call-done = bf16[256,5120]{1,0:T(8,128)(2,1)} async-done(((bf16[32,5120]{1,0:T(8,128)(2,1)}), bf16[256,5120]{1,0:T(8,128)(2,1)}) %all-gather.10.cloned.1.call-update) | async-done | bytes 2621456 | tf_op jit(solution)/shard_map/all_gather | solution.py:95
  197.2 2.8 convolution_convert_fusion.9
  199.9 0.8 copy.28
  200.7 4.0 %all-to-all-start.2 = ((bf16[8,32,160]{2,1,0:T(8,128)(2,1)}), bf16[8,32,160]{2,1,0:T(8,128)(2,1)S(1)}, u32[]{:S(2)}, u32[]{:S(2)}) async-start(bf16[8,32,160]{2,1,0:T(8,128)(2,1)} %bitcast.19), calls=%async_computation.2 | async-start | bytes 262144 | tf_op jit(solution)/shard_map/all_to_all | solution.py:98
  204.7 0.7 sub.70
  205.5 7.2 %all-to-all-done.2 = bf16[8,32,160]{2,1,0:T(8,128)(2,1)S(1)} async-done(((bf16[8,32,160]{2,1,0:T(8,128)(2,1)}), bf16[8,32,160]{2,1,0:T(8,128)(2,1)S(1)}, u32[]{:S(2)}, u32[]{:S(2)}) %all-to-all-start.2) | async-done | bytes 81952 | tf_op jit(solution)/shard_map/all_to_all | solution.py:98
  212.6 15.5 %all-to-all-start = ((s32[64,1,2]{2,1,0:T(1,128)}), s32[64,1,2]{2,1,0:T(1,128)S(1)}, u32[]{:S(2)}, u32[]{:S(2)}) async-start(s32[64,1,2]{2,1,0:T(1,128)} %bitcast), calls=%async_computation | async-start | bytes 65536 | tf_op jit(solution)/shard_map/all_to_all | solution.py:119
  228.8 0.8 reshape.289
  229.6 7.8 %all-to-all-done = s32[64,1,2]{2,1,0:T(1,128)S(1)} async-done(((s32[64,1,2]{2,1,0:T(1,128)}), s32[64,1,2]{2,1,0:T(1,128)S(1)}, u32[]{:S(2)}, u32[]{:S(2)}) %all-to-all-start) | async-done | bytes 544 | tf_op jit(solution)/shard_map/all_to_all | solution.py:119
  237.5 4.9 %all-to-all-start.3 = ((bf16[64,2,1280]{2,1,0:T(2,128)(2,1)}), bf16[64,2,1280]{2,1,0:T(2,128)(2,1)S(1)}, u32[]{:S(2)}, u32[]{:S(2)}) async-start(bf16[64,2,1280]{2,1,0:T(2,128)(2,1)} %reshape.289), calls=%async_computation.3 | async-start | bytes 655360 | tf_op jit(solution)/shard_map/all_to_all | solution.py:118
  243.0 0.8 reduce.3
  244.1 11.7 %all-to-all-done.3 = bf16[64,2,1280]{2,1,0:T(2,128)(2,1)S(1)} async-done(((bf16[64,2,1280]{2,1,0:T(2,128)(2,1)}), bf16[64,2,1280]{2,1,0:T(2,128)(2,1)S(1)}, u32[]{:S(2)}, u32[]{:S(2)}) %all-to-all-start.3) | async-done | bytes 327712 | tf_op jit(solution)/shard_map/all_to_all | solution.py:118
  256.5 0.9 multiply_convert_fusion
  258.0 10.6 %all_gather.31 = s32[1,1024]{1,0:T(1,128)S(1)} all-gather(s32[1,128]{1,0:T(1,128)S(1)} %copy-done.6), channel_id=1, replica_groups=mesh['grp'=64,'tp'=8] {'tp'}, dimensions={1}, use_global_device_ids=true | all-gather | bytes 4608 | tf_op jit(solution)/shard_map/all_gather | solution.py:132
  269.4 21.1 %all-gather.12.cloned.1.call-done = bf16[1024,1280]{1,0:T(8,128)(2,1)} async-done(((bf16[128,1280]{1,0:T(8,128)(2,1)}), bf16[1024,1280]{1,0:T(8,128)(2,1)}) %all-gather.12.cloned.1.call-update) | async-done | bytes 2621456 | tf_op jit(solution)/shard_map/all_gather | solution.py:131
  290.5 2.9 convolution_convert_fusion.4
  293.5 0.7 slice.97
  294.2 1.0 convolution_convert_fusion.2
  295.2 0.7 slice.100
  295.9 1.0 convolution_convert_fusion.3
  297.0 2.0 fusion.84
  299.0 2.3 convolution_convert_fusion.8
  301.3 4.6 %fusion.83 = (f32[2,512]{1,0:T(2,128)S(1)}, f32[2,512,1024]{2,1,0:T(8,128)}) fusion(pred[512,1024]{1,0:T(8,128)(4,1)S(1)} %fusion.18, bf16[512,2,80]{0,2,1:T(8,128)(2,1)S(1)} %bitcast.110, bf16[1024,2,80]{0,2,1:T(8,128)(2,1)} %bitcast.121), kind=kOutput, calls=%fused_computation.135 | convolution fusion | flops 171967488 | bytes 5214208 | tf_op jit(solution)/shard_map/sub | solution.py:55
  305.9 3.1 fusion.26
  309.0 0.8 copy_bitcast_fusion
  309.8 4.0 all-to-all-start.4
  313.8 66.9 %all-gather.16.cloned.1.call-done = bf16[64,20,1280]{2,1,0:T(8,128)(2,1)} async-done(((bf16[1,20,1280]{2,1,0:T(8,128)(2,1)}), bf16[64,20,1280]{2,1,0:T(8,128)(2,1)}) %all-gather.16.cloned.1.call-update) | async-done | bytes 3276816 | tf_op jit(solution)/shard_map/all_gather | solution.py:74
  380.7 6.1 %reshape.298 = bf16[1280,1280]{1,0:T(8,128)(2,1)} reshape(bf16[64,20,1280]{2,1,0:T(8,128)(2,1)} %all-gather.16.cloned.1.call-done) | data formatting | bytes 6553600
  386.8 3.9 fusion.8
  (67 shorter events, 5.4 us)
Async XLA Ops:
  6.5 190.6 %copy-start = (bf16[160,5120]{1,0:T(8,128)(2,1)S(1)}, bf16[160,5120]{1,0:T(8,128)(2,1)}, u32[]{:S(2)}) copy-start(bf16[160,5120]{1,0:T(8,128)(2,1)} %param.14) | copy-start | bytes 4915204
  6.5 51.5 %all-gather.8.cloned.1.call-start = ((), (), s32[]{:S(2)}) async-start(), calls=%async_computation.5 | async-start | bytes 2949120 | tf_op jit(solution)/shard_map/all_gather | solution.py:86
  10.9 137.5 %all-gather.14.cloned.1.call-start = ((), (), s32[]{:S(2)}) async-start(), calls=%async_computation.8 | async-start | bytes 3993600 | tf_op jit(solution)/shard_map/all_gather | solution.py:74
  58.0 3.0 copy-start.7
  58.0 3.0 copy-start.9
  73.0 3.4 copy-start.12
  78.1 76.4 %all-to-all-start.1 = ((bf16[8,128,160]{1,2,0:T(8,128)(2,1)}), bf16[8,128,160]{1,2,0:T(8,128)(2,1)S(1)}, u32[]{:S(2)}, u32[]{:S(2)}) async-start(bf16[8,128,160]{1,2,0:T(8,128)(2,1)} %copy_bitcast_fusion.1), calls=%async_computation.1 | async-start | bytes 655360 | tf_op jit(solution)/shard_map/all_to_all | solution.py:90
  82.1 72.4 %copy-start.1 = (bf16[128,1280]{1,0:T(8,128)(2,1)S(1)}, bf16[128,1280]{1,0:T(8,128)(2,1)}, u32[]{:S(2)}) copy-start(bf16[128,1280]{1,0:T(8,128)(2,1)} %param.10) | copy-start | bytes 983044
  82.1 115.1 %all-gather.10.cloned.1.call-start = ((), (), s32[]{:S(2)}) async-start(), calls=%async_computation.6 | async-start | bytes 2949120 | tf_op jit(solution)/shard_map/all_gather | solution.py:95
  154.5 4.6 %copy-start.11 = (s32[32]{0:T(128)S(1)}, s32[32]{0:T(128)}, u32[]{:S(2)}) copy-start(s32[32]{0:T(128)} %param.16) | copy-start | bytes 388
  199.9 56.0 %copy-start.2 = (bf16[128,1280]{1,0:T(8,128)(2,1)S(1)}, bf16[128,1280]{1,0:T(8,128)(2,1)}, u32[]{:S(2)}) copy-start(bf16[128,1280]{1,0:T(8,128)(2,1)} %param.15) | copy-start | bytes 983044
  200.7 12.0 %all-to-all-start.2 = ((bf16[8,32,160]{2,1,0:T(8,128)(2,1)}), bf16[8,32,160]{2,1,0:T(8,128)(2,1)S(1)}, u32[]{:S(2)}, u32[]{:S(2)}) async-start(bf16[8,32,160]{2,1,0:T(8,128)(2,1)} %bitcast.19), calls=%async_computation.2 | async-start | bytes 262144 | tf_op jit(solution)/shard_map/all_to_all | solution.py:98
  212.6 24.8 %all-to-all-start = ((s32[64,1,2]{2,1,0:T(1,128)}), s32[64,1,2]{2,1,0:T(1,128)S(1)}, u32[]{:S(2)}, u32[]{:S(2)}) async-start(s32[64,1,2]{2,1,0:T(1,128)} %bitcast), calls=%async_computation | async-start | bytes 65536 | tf_op jit(solution)/shard_map/all_to_all | solution.py:119
  228.8 29.2 %copy-start.6 = (s32[1,128]{1,0:T(1,128)S(1)}, s32[1,128]{1,0:T(1,128)}, u32[]{:S(2)}) copy-start(s32[1,128]{1,0:T(1,128)} %param.17) | copy-start | bytes 1540
  237.5 18.3 %all-to-all-start.3 = ((bf16[64,2,1280]{2,1,0:T(2,128)(2,1)}), bf16[64,2,1280]{2,1,0:T(2,128)(2,1)S(1)}, u32[]{:S(2)}, u32[]{:S(2)}) async-start(bf16[64,2,1280]{2,1,0:T(2,128)(2,1)} %reshape.289), calls=%async_computation.3 | async-start | bytes 655360 | tf_op jit(solution)/shard_map/all_to_all | solution.py:118
  242.4 48.1 %all-gather.12.cloned.1.call-start = ((), (), s32[]{:S(2)}) async-start(), calls=%async_computation.7 | async-start | bytes 2949120 | tf_op jit(solution)/shard_map/all_gather | solution.py:131
  257.4 123.4 %all-gather.16.cloned.1.call-start = ((), (), s32[]{:S(2)}) async-start(), calls=%async_computation.9 | async-start | bytes 3993600 | tf_op jit(solution)/shard_map/all_gather | solution.py:74
  290.5 3.7 copy-start.8
  290.5 3.7 copy-start.10
  293.4 1.7 copy-start.4
  295.2 1.7 copy-start.5
  297.0 2.0 copy-start.3
  309.8 77.0 %all-to-all-start.4 = ((bf16[8,128,160]{1,2,0:T(8,128)(2,1)}), bf16[8,128,160]{1,2,0:T(8,128)(2,1)S(1)}, u32[]{:S(2)}, u32[]{:S(2)}) async-start(bf16[8,128,160]{1,2,0:T(8,128)(2,1)} %copy_bitcast_fusion), calls=%async_computation.4 | async-start | bytes 655360 | tf_op jit(solution)/shard_map/all_to_all | solution.py:135
Sparse Core Ops, SparseCore 0:
  11.0 46.9 all-gather.7
  61.3 87.0 all-gather.13
  159.2 37.8 all-gather.9
  257.5 32.9 all-gather.11
  293.6 87.0 all-gather.15
where the time goes:
time: 398 us; the launch traced here: 397 us
  waiting for transfers between devices  252 us (63%)
  matrix products  46.3 us (12%)
  starting transfers between devices  32.6 us (8%)
  blocking collectives  24.6 us (6%)
  local copies, waits for them, and re-layouts  18.4 us (5%)
  between operations  13.5 us (3%)
  other arithmetic  10 us (3%)
    all_gather x2, waiting for transfers between devices, project_out(): lax.all_gather(columns, 'grp', axis=1, tiled=True)  133 us
    all_gather x1, waiting for transfers between devices, per_device(): lax.all_gather(merged, 'tp', axis=0, tiled=True)  37.7 us
    all_gather x1, waiting for transfers between devices, per_device(): lax.all_gather(patch_normed, 'tp', axis=0, tiled=True)  31.7 us
    all_gather x1, waiting for transfers between devices, per_device(): lax.all_gather(token_normed, 'tp', axis=0, tiled=True)  21.1 us
    sub x4, matrix products, local_attention(): weights = jnp.exp(scores - row_max)  15.8 us
    all_to_all x1, starting transfers between devices, per_device(): lax.all_to_all(send_pos, 'grp', split_axis=0, concat_axis=0, tiled=True)  15.5 us
    all_gather x1, blocking collectives, per_device(): lax.all_gather(pictures, 'tp', axis=1, tiled=True)  14 us
    dot_general x7, matrix products, times_transpose(): lax.dot_general(left, right, (((1,), (1,)), ((), ())), preferred_element_...  13.3 us
  transfers between devices with their start and end apart: 10, of which 8 were waited for; matrix products, arithmetic and copies ran while one was open for 14% of the time, Pallas kernels for 0%

commit v1 on v0

--- a/solution.py
+++ b/solution.py
@@ -128,7 +128,9 @@
     prompt = jnp.where(covered[:, None], placed, text)
     token_normed = layer_norm(prompt)
     all_tokens, all_segments = (
-        lax.all_gather(token_normed, "tp", axis=0, tiled=True),
+        jnp.concatenate(
+            lax.all_to_all(jnp.stack([token_normed] * lax.axis_size("tp")), "tp", 0, 0), axis=0
+        ),
         lax.all_gather(segments, "tp", axis=1, tiled=True),
     )
     heads_txt = attention_heads(all_tokens, txt_qkv, all_segments[0], True)

time: 398 us -> 383 us (0.962)
  waiting for transfers between devices: 252 us -> 168 us
  blocking collectives: 24.6 us -> 80.9 us
  starting transfers between devices: 32.6 us -> 37.8 us
    all_gather x2, waiting for transfers between devices: 133 us -> 66.3 us  [project_out(): lax.all_gather(columns, 'grp', axis=1, tiled=True)]
    all_gather x1, blocking collectives: 10.6 us -> 66.9 us  [per_device(): lax.all_gather(segments, 'tp', axis=1, tiled=True)]
    all_gather x1 -> x0, waiting for transfers between devices: 21.1 us -> none  [per_device(): lax.all_gather(token_normed, 'tp', axis=0, tiled=True)]
    all_to_all x0 -> x1, starting transfers between devices: none -> 4.51 us  [per_device(): lax.all_to_all(jnp.stack([token_normed] * lax.axis_size('tp')), 'tp', 0, 0)]
    all_to_all x1, waiting for transfers between devices: 0.01 us -> 4.18 us  [per_device(): lax.all_to_all(heads_txt, 'tp', split_axis=0, concat_axis=1, tiled=True)]
    unnamed x28 -> x26, local copies, waits for them, and re-layouts: 12.6 us -> 12.6 us
  transfers between devices with their start and end apart: 10 -> 10, of which waited for: 8 -> 7; matrix products, arithmetic and copies ran while one was open for 14% -> 16% of each run, Pallas kernels for 0% -> 0%
where the time goes in v1:
time: 383 us; the launch traced here: 379 us
  waiting for transfers between devices  168 us (44%)
  blocking collectives  80.9 us (21%)
  matrix products  49.9 us (13%)
  starting transfers between devices  37.8 us (10%)
  local copies, waits for them, and re-layouts  20.2 us (5%)
  between operations  13.5 us (4%)
  other arithmetic  9.3 us (2%)
    all_gather x1, blocking collectives, per_device(): lax.all_gather(segments, 'tp', axis=1, tiled=True)  66.9 us
    all_gather x2, waiting for transfers between devices, project_out(): lax.all_gather(columns, 'grp', axis=1, tiled=True)  66.3 us
    all_gather x1, waiting for transfers between devices, per_device(): lax.all_gather(merged, 'tp', axis=0, tiled=True)  37.7 us
    all_gather x1, waiting for transfers between devices, per_device(): lax.all_gather(patch_normed, 'tp', axis=0, tiled=True)  31.7 us
    dot_general x7, matrix products, times_transpose(): lax.dot_general(left, right, (((1,), (1,)), ((), ())), preferred_element_...  16.9 us
    sub x4, matrix products, local_attention(): weights = jnp.exp(scores - row_max)  15.8 us
    all_to_all x1, starting transfers between devices, per_device(): lax.all_to_all(send_pos, 'grp', split_axis=0, concat_axis=0, tiled=True)  15.5 us
    all_gather x1, blocking collectives, per_device(): lax.all_gather(pictures, 'tp', axis=1, tiled=True)  14 us
  transfers between devices with their start and end apart: 10, of which 7 were waited for; matrix products, arithmetic and copies ran while one was open for 16% of the time, Pallas kernels for 0%

profile of v1, /device:TPU:1, one launch (start us, length us, event | category | flops | bytes accessed | tf_op | source)
XLA Modules:
  0.0 379.4 jit_solution(4563801953519058728)
XLA Ops:
  6.5 1.2 convert_reduce_fusion
  7.8 1.2 fusion.35
  9.0 1.9 fusion.36
  11.0 0.7 all-gather.11.cloned.1.call-update
  11.7 14.0 %all_gather.23 = s32[1,1024]{1,0:T(1,128)S(1)} all-gather(s32[1,128]{1,0:T(1,128)} %param.11), channel_id=1, replica_groups=mesh['grp'=64,'tp'=8] {'tp'}, dimensions={1}, use_global_device_ids=true | all-gather | bytes 4608 | tf_op jit(solution)/shard_map/all_gather | solution.py:87
  26.3 31.7 %all-gather.7.cloned.1.call-done = bf16[1024,1280]{1,0:T(8,128)(2,1)} async-done(((bf16[128,1280]{1,0:T(8,128)(2,1)}), bf16[1024,1280]{1,0:T(8,128)(2,1)}) %all-gather.7.cloned.1.call-update) | async-done | bytes 2621456 | tf_op jit(solution)/shard_map/all_gather | solution.py:86
  58.0 2.9 convolution_convert_fusion.6
  61.0 1.0 convolution_convert_fusion.7
  62.0 1.7 convolution_convert_fusion.5
  63.7 4.6 %fusion.79 = (f32[2,512]{1,0:T(2,128)S(1)}, f32[2,512,1024]{2,1,0:T(8,128)}) fusion(pred[512,1024]{1,0:T(8,128)(4,1)S(1)} %get-tuple-element.12, bf16[512,2,80]{0,2,1:T(8,128)(2,1)S(1)} %bitcast.112, bf16[1024,2,80]{0,2,1:T(8,128)(2,1)} %bitcast.133), kind=kOutput, calls=%fused_computation.131 | convolution fusion | flops 171967488 | bytes 5214208 | tf_op jit(solution)/shard_map/sub | solution.py:55
  68.3 4.6 %fusion.80 = (f32[2,512]{1,0:T(2,128)S(1)}, f32[2,512,1024]{2,1,0:T(8,128)}) fusion(pred[512,1024]{1,0:T(8,128)(4,1)S(1)} %get-tuple-element.11, bf16[512,2,80]{0,2,1:T(8,128)(2,1)S(1)} %bitcast.110, bf16[1024,2,80]{0,2,1:T(8,128)(2,1)} %bitcast.134), kind=kOutput, calls=%fused_computation.132 | convolution fusion | flops 171967488 | bytes 5214208 | tf_op jit(solution)/shard_map/sub | solution.py:55
  73.0 3.2 fusion.27
  76.4 0.8 fusion.28
  77.3 0.8 copy_bitcast_fusion.1
  78.1 4.0 %all-to-all-start.1 = ((bf16[8,128,160]{1,2,0:T(8,128)(2,1)}), bf16[8,128,160]{1,2,0:T(8,128)(2,1)S(1)}, u32[]{:S(2)}, u32[]{:S(2)}) async-start(bf16[8,128,160]{1,2,0:T(8,128)(2,1)} %copy_bitcast_fusion.1), calls=%async_computation.1 | async-start | bytes 655360 | tf_op jit(solution)/shard_map/all_to_all | solution.py:90
  82.1 66.2 %all-gather.11.cloned.1.call-done = bf16[64,20,1280]{2,1,0:T(8,128)(2,1)} async-done(((bf16[1,20,1280]{2,1,0:T(8,128)(2,1)}), bf16[64,20,1280]{2,1,0:T(8,128)(2,1)}) %all-gather.11.cloned.1.call-update) | async-done | bytes 3276816 | tf_op jit(solution)/shard_map/all_gather | solution.py:74
  148.4 6.1 %reshape.302 = bf16[1280,1280]{1,0:T(8,128)(2,1)} reshape(bf16[64,20,1280]{2,1,0:T(8,128)(2,1)} %all-gather.11.cloned.1.call-done) | data formatting | bytes 6553600
  154.5 3.2 fusion.81
  158.1 0.9 reshape.293
  159.4 37.7 %all-gather.9.cloned.1.call-done = bf16[256,5120]{1,0:T(8,128)(2,1)} async-done(((bf16[32,5120]{1,0:T(8,128)(2,1)}), bf16[256,5120]{1,0:T(8,128)(2,1)}) %all-gather.9.cloned.1.call-update) | async-done | bytes 2621456 | tf_op jit(solution)/shard_map/all_gather | solution.py:95
  197.2 2.8 convolution_convert_fusion.9
  199.9 0.8 copy.28
  200.7 4.0 %all-to-all-start.2 = ((bf16[8,32,160]{2,1,0:T(8,128)(2,1)}), bf16[8,32,160]{2,1,0:T(8,128)(2,1)S(1)}, u32[]{:S(2)}, u32[]{:S(2)}) async-start(bf16[8,32,160]{2,1,0:T(8,128)(2,1)} %bitcast.19), calls=%async_computation.2 | async-start | bytes 262144 | tf_op jit(solution)/shard_map/all_to_all | solution.py:98
  204.7 0.7 sub.70
  205.5 7.2 %all-to-all-done.2 = bf16[8,32,160]{2,1,0:T(8,128)(2,1)S(1)} async-done(((bf16[8,32,160]{2,1,0:T(8,128)(2,1)}), bf16[8,32,160]{2,1,0:T(8,128)(2,1)S(1)}, u32[]{:S(2)}, u32[]{:S(2)}) %all-to-all-start.2) | async-done | bytes 81952 | tf_op jit(solution)/shard_map/all_to_all | solution.py:98
  212.6 15.5 %all-to-all-start = ((s32[64,1,2]{2,1,0:T(1,128)}), s32[64,1,2]{2,1,0:T(1,128)S(1)}, u32[]{:S(2)}, u32[]{:S(2)}) async-start(s32[64,1,2]{2,1,0:T(1,128)} %bitcast), calls=%async_computation | async-start | bytes 65536 | tf_op jit(solution)/shard_map/all_to_all | solution.py:119
  228.8 0.9 reshape.294
  229.6 7.8 %all-to-all-done = s32[64,1,2]{2,1,0:T(1,128)S(1)} async-done(((s32[64,1,2]{2,1,0:T(1,128)}), s32[64,1,2]{2,1,0:T(1,128)S(1)}, u32[]{:S(2)}, u32[]{:S(2)}) %all-to-all-start) | async-done | bytes 544 | tf_op jit(solution)/shard_map/all_to_all | solution.py:119
  237.5 4.9 %all-to-all-start.3 = ((bf16[64,2,1280]{2,1,0:T(2,128)(2,1)}), bf16[64,2,1280]{2,1,0:T(2,128)(2,1)S(1)}, u32[]{:S(2)}, u32[]{:S(2)}) async-start(bf16[64,2,1280]{2,1,0:T(2,128)(2,1)} %reshape.294), calls=%async_computation.3 | async-start | bytes 655360 | tf_op jit(solution)/shard_map/all_to_all | solution.py:118
  243.0 0.8 reduce.3
  244.0 11.7 %all-to-all-done.3 = bf16[64,2,1280]{2,1,0:T(2,128)(2,1)S(1)} async-done(((bf16[64,2,1280]{2,1,0:T(2,128)(2,1)}), bf16[64,2,1280]{2,1,0:T(2,128)(2,1)S(1)}, u32[]{:S(2)}, u32[]{:S(2)}) %all-to-all-start.3) | async-done | bytes 327712 | tf_op jit(solution)/shard_map/all_to_all | solution.py:118
  256.6 1.7 stack.2
  258.3 4.5 %all-to-all-start.4 = ((bf16[8,128,1280]{2,1,0:T(8,128)(2,1)}), bf16[8,128,1280]{2,1,0:T(8,128)(2,1)}, u32[]{:S(2)}, u32[]{:S(2)}) async-start(bf16[8,128,1280]{2,1,0:T(8,128)(2,1)} %stack.2), calls=%async_computation.4 | async-start | bytes 5242880 | tf_op jit(solution)/shard_map/all_to_all | solution.py:132
  263.4 66.9 %all_gather.27 = s32[1,1024]{1,0:T(1,128)S(1)} all-gather(s32[1,128]{1,0:T(1,128)S(1)} %copy-done.6), channel_id=1, replica_groups=mesh['grp'=64,'tp'=8] {'tp'}, dimensions={1}, use_global_device_ids=true | all-gather | bytes 4608 | tf_op jit(solution)/shard_map/all_gather | solution.py:134
  331.2 2.9 convolution_convert_fusion.4
  334.1 0.7 slice.97
  334.9 2.8 convolution_convert_fusion.2
  337.6 0.7 slice.100
  338.4 2.8 convolution_convert_fusion.3
  341.2 2.0 fusion.84
  343.2 2.3 convolution_convert_fusion.8
  345.5 4.6 %fusion.83 = (f32[2,512]{1,0:T(2,128)S(1)}, f32[2,512,1024]{2,1,0:T(8,128)}) fusion(pred[512,1024]{1,0:T(8,128)(4,1)S(1)} %fusion.18, bf16[512,2,80]{0,2,1:T(8,128)(2,1)S(1)} %bitcast.111, bf16[1024,2,80]{0,2,1:T(8,128)(2,1)} %bitcast.122), kind=kOutput, calls=%fused_computation.135 | convolution fusion | flops 171967488 | bytes 5214208 | tf_op jit(solution)/shard_map/sub | solution.py:55
  350.1 3.1 fusion.26
  353.2 0.8 copy_bitcast_fusion
  354.0 4.7 %all-to-all-start.5 = ((bf16[8,128,160]{1,2,0:T(8,128)(2,1)}), bf16[8,128,160]{1,2,0:T(8,128)(2,1)S(1)}, u32[]{:S(2)}, u32[]{:S(2)}) async-start(bf16[8,128,160]{1,2,0:T(8,128)(2,1)} %copy_bitcast_fusion), calls=%async_computation.5 | async-start | bytes 655360 | tf_op jit(solution)/shard_map/all_to_all | solution.py:137
  358.7 6.1 %reshape.304 = bf16[1280,1280]{1,0:T(8,128)(2,1)} reshape(bf16[64,20,1280]{2,1,0:T(8,128)(2,1)} %all-gather.13.cloned.1.call-done) | data formatting | bytes 6553600
  364.8 4.2 %all-to-all-done.5 = bf16[8,128,160]{1,2,0:T(8,128)(2,1)S(1)} async-done(((bf16[8,128,160]{1,2,0:T(8,128)(2,1)}), bf16[8,128,160]{1,2,0:T(8,128)(2,1)S(1)}, u32[]{:S(2)}, u32[]{:S(2)}) %all-to-all-start.5) | async-done | bytes 327712 | tf_op jit(solution)/shard_map/all_to_all | solution.py:137
  369.0 3.9 %fusion.8 = bf16[128,1280]{1,0:T(8,128)(2,1)} fusion(f32[128,1280]{1,0:T(8,128)S(1)} %get-tuple-element.24, bf16[128,1280]{0,1:T(8,128)(2,1)S(1)} %bitcast.107, bf16[1280,1280]{1,0:T(8,128)(2,1)} %reshape.304), kind=kOutput, calls=%fused_computation.19 | convolution fusion | flops 419758080 | bytes 4587520 | tf_op jit(solution)/shard_map/dot_general | solution.py:72
  (65 shorter events, 5.5 us)
Async XLA Ops:
  6.5 190.6 %copy-start = (bf16[160,5120]{1,0:T(8,128)(2,1)S(1)}, bf16[160,5120]{1,0:T(8,128)(2,1)}, u32[]{:S(2)}) copy-start(bf16[160,5120]{1,0:T(8,128)(2,1)} %param.14) | copy-start | bytes 4915204
  6.5 51.5 %all-gather.7.cloned.1.call-start = ((), (), s32[]{:S(2)}) async-start(), calls=%async_computation.6 | async-start | bytes 2949120 | tf_op jit(solution)/shard_map/all_gather | solution.py:86
  10.9 137.5 %all-gather.11.cloned.1.call-start = ((), (), s32[]{:S(2)}) async-start(), calls=%async_computation.8 | async-start | bytes 3993600 | tf_op jit(solution)/shard_map/all_gather | solution.py:74
  58.0 3.0 copy-start.7
  58.0 3.0 copy-start.8
  73.0 3.4 copy-start.11
  78.1 76.4 %all-to-all-start.1 = ((bf16[8,128,160]{1,2,0:T(8,128)(2,1)}), bf16[8,128,160]{1,2,0:T(8,128)(2,1)S(1)}, u32[]{:S(2)}, u32[]{:S(2)}) async-start(bf16[8,128,160]{1,2,0:T(8,128)(2,1)} %copy_bitcast_fusion.1), calls=%async_computation.1 | async-start | bytes 655360 | tf_op jit(solution)/shard_map/all_to_all | solution.py:90
  82.1 72.4 %copy-start.1 = (bf16[128,1280]{1,0:T(8,128)(2,1)S(1)}, bf16[128,1280]{1,0:T(8,128)(2,1)}, u32[]{:S(2)}) copy-start(bf16[128,1280]{1,0:T(8,128)(2,1)} %param.10) | copy-start | bytes 983044
  82.1 115.1 %all-gather.9.cloned.1.call-start = ((), (), s32[]{:S(2)}) async-start(), calls=%async_computation.7 | async-start | bytes 2949120 | tf_op jit(solution)/shard_map/all_gather | solution.py:95
  154.5 4.6 %copy-start.10 = (s32[32]{0:T(128)S(1)}, s32[32]{0:T(128)}, u32[]{:S(2)}) copy-start(s32[32]{0:T(128)} %param.16) | copy-start | bytes 388
  199.9 56.0 %copy-start.2 = (bf16[128,1280]{1,0:T(8,128)(2,1)S(1)}, bf16[128,1280]{1,0:T(8,128)(2,1)}, u32[]{:S(2)}) copy-start(bf16[128,1280]{1,0:T(8,128)(2,1)} %param.15) | copy-start | bytes 983044
  200.7 12.0 %all-to-all-start.2 = ((bf16[8,32,160]{2,1,0:T(8,128)(2,1)}), bf16[8,32,160]{2,1,0:T(8,128)(2,1)S(1)}, u32[]{:S(2)}, u32[]{:S(2)}) async-start(bf16[8,32,160]{2,1,0:T(8,128)(2,1)} %bitcast.19), calls=%async_computation.2 | async-start | bytes 262144 | tf_op jit(solution)/shard_map/all_to_all | solution.py:98
  212.6 24.8 %all-to-all-start = ((s32[64,1,2]{2,1,0:T(1,128)}), s32[64,1,2]{2,1,0:T(1,128)S(1)}, u32[]{:S(2)}, u32[]{:S(2)}) async-start(s32[64,1,2]{2,1,0:T(1,128)} %bitcast), calls=%async_computation | async-start | bytes 65536 | tf_op jit(solution)/shard_map/all_to_all | solution.py:119
  237.5 18.3 %all-to-all-start.3 = ((bf16[64,2,1280]{2,1,0:T(2,128)(2,1)}), bf16[64,2,1280]{2,1,0:T(2,128)(2,1)S(1)}, u32[]{:S(2)}, u32[]{:S(2)}) async-start(bf16[64,2,1280]{2,1,0:T(2,128)(2,1)} %reshape.294), calls=%async_computation.3 | async-start | bytes 655360 | tf_op jit(solution)/shard_map/all_to_all | solution.py:118
  258.3 5.1 %copy-start.6 = (s32[1,128]{1,0:T(1,128)S(1)}, s32[1,128]{1,0:T(1,128)}, u32[]{:S(2)}) copy-start(s32[1,128]{1,0:T(1,128)} %param.17) | copy-start | bytes 1540
  258.3 72.8 %all-to-all-start.4 = ((bf16[8,128,1280]{2,1,0:T(8,128)(2,1)}), bf16[8,128,1280]{2,1,0:T(8,128)(2,1)}, u32[]{:S(2)}, u32[]{:S(2)}) async-start(bf16[8,128,1280]{2,1,0:T(8,128)(2,1)} %stack.2), calls=%async_computation.4 | async-start | bytes 5242880 | tf_op jit(solution)/shard_map/all_to_all | solution.py:132
  262.9 95.8 %all-gather.13.cloned.1.call-start = ((), (), s32[]{:S(2)}) async-start(), calls=%async_computation.9 | async-start | bytes 3993600 | tf_op jit(solution)/shard_map/all_gather | solution.py:74
  331.2 3.7 copy-start.9
  334.1 3.5 copy-start.4
  337.6 3.5 copy-start.5
  341.2 2.0 copy-start.3
  354.0 15.0 %all-to-all-start.5 = ((bf16[8,128,160]{1,2,0:T(8,128)(2,1)}), bf16[8,128,160]{1,2,0:T(8,128)(2,1)S(1)}, u32[]{:S(2)}, u32[]{:S(2)}) async-start(bf16[8,128,160]{1,2,0:T(8,128)(2,1)} %copy_bitcast_fusion), calls=%async_computation.5 | async-start | bytes 655360 | tf_op jit(solution)/shard_map/all_to_all | solution.py:137
Sparse Core Ops, SparseCore 0:
  11.0 46.9 all-gather.6
  61.3 87.0 all-gather.10
  159.2 37.8 all-gather.8
  266.6 82.2 all-gather.12
